TPU v7x, 128 devices: a whole 4x4x4 slice. The times are simulated.
128 devices in a mesh: gx: 16 (over z_lo, x, core), gy: 8 (over z_hi, y).
Axes of the slice: x: 4, y: 4, z: 4 (z_hi: 2, z_lo: 2; z = z_hi * 2 + z_lo), core: 2. Of those that a mesh axis runs over, the one named last changes fastest.
Arguments:
- scalar: float32 [1024, 512, 512], P('gx', 'gy'), may hold values from -6 to 6
- prefactor: float32 [1024, 512, 512], P('gx', 'gy'), may hold values from 0.05 to 1
- factor_x: float32 [1024, 512], P('gx'), may hold values from -0.25 to 0.25
- factor_y: float32 [512, 64], P('gy'), may hold values from -0.375 to 0.375
- factor_z: bfloat16 [512, 128], replicated, may hold values from -0.25 to 0.25
Outputs:
- advanced: float32 [1024, 512, 512], P('gx', 'gy')
- core: float32 [512, 64, 128], P('gx', 'gy')
All inputs are finite; a program needn't handle non-finite values.
Results may differ from a plain program's by a relative error of at most 0.0029.
Values sent between devices are 32-bit elements; how exact they have to be, the bound alone decides.
A program may use at most 128 MiB of HBM per device.

v0:
```python
import jax
import jax.numpy as jnp
from jax import lax
from jax.sharding import PartitionSpec as P

spread_rate = 0.12
activation = 2.0


def extended(array, sides, width):
    edges = {}
    for axis, dim in sides:
        peers, length = (lax.axis_size(axis), array.shape[dim])
        up = [(i, (i + 1) % peers) for i in range(peers - 1)]
        last = lax.slice_in_dim(array, length - width, length, axis=dim)
        first = lax.slice_in_dim(array, 0, width, axis=dim)
        edges[dim] = (
            lax.ppermute(last, axis, up),
            lax.ppermute(first, axis, [(b, a) for a, b in up]),
        )
    done = []
    for _, dim in sides:
        low, high = edges[dim]
        around = [(width, width) if d in done else (0, 0) for d in range(array.ndim)]
        array = jnp.concatenate([jnp.pad(low, around), array, jnp.pad(high, around)], axis=dim)
        done.append(dim)
    return array


def in_blocks(array, dim, peers):
    before, after = (array.shape[:dim], array.shape[dim + 1 :])
    return jnp.moveaxis(array.reshape(*before, peers, -1, *after), dim, 0)


def sent_and_summed(array, axis, dim):
    peers = lax.axis_size(axis)
    blocks = lax.all_to_all(in_blocks(array, dim, peers), axis, 0, 0, tiled=True)
    return jnp.sum(blocks, axis=0)


def laplace(padded):
    center = padded[1:-1, 1:-1]
    z_padded = jnp.pad(center, ((0, 0), (0, 0), (1, 1)))
    beside = padded[2:, 1:-1] + padded[:-2, 1:-1] + padded[1:-1, 2:] + padded[1:-1, :-2]
    beside = beside + z_padded[:, :, 2:] + z_padded[:, :, :-2]
    return beside - 6.0 * center


def sources(field, prefactor):
    return prefactor * jnp.exp(-activation / (1.0 + field * field))


def section_rate(field, prefactor):
    padded = extended(field, (("gx", 0), ("gy", 1)), 1)
    return spread_rate * laplace(padded) + sources(field, prefactor)


def on_device(scalar, prefactor, factor_x, factor_y, factor_z):
    cells_x, cells_y, depth = scalar.shape
    first = section_rate(scalar, prefactor)
    middle = scalar + first
    second = section_rate(middle, prefactor)
    advanced = scalar + 0.5 * (first + second)
    lowered = advanced.astype(jnp.bfloat16)
    z_reduced = jnp.dot(
        lowered.reshape(cells_x * cells_y, depth), factor_z, preferred_element_type=jnp.float32
    ).reshape(cells_x, cells_y, -1)
    y_reduced = jnp.einsum("xyc,yb->xbc", z_reduced, factor_y, precision=lax.Precision.HIGHEST)
    y_owned = sent_and_summed(y_reduced, "gy", 1)
    core = sent_and_summed(
        jnp.einsum("xa,xbc->abc", factor_x, y_owned, precision=lax.Precision.HIGHEST), "gx", 0
    )
    return (advanced, core)


def solution(mesh):
    return jax.shard_map(
        on_device,
        mesh=mesh,
        in_specs=(P("gx", "gy", None), P("gx", "gy", None), P("gx", None), P("gy", None), P()),
        out_specs=(P("gx", "gy", None), P("gx", "gy", None)),
        check_vma=False,
    )
```

profile of v0, /device:TPU:1, one launch (start us, length us, event | category | flops | bytes accessed | tf_op | source)
XLA Modules:
  0.0 187.8 jit_solution(17056847219280291526)
XLA Ops:
  0.6 0.0 copy-start
  0.6 1.0 fusion.32
  1.7 4.5 %collective-permute-start.1 = (f32[1,64,512]{2,1,0:T(8,128)S(1)}, f32[1,64,512]{2,1,0:T(8,128)S(1)}, u32[]{:S(2)}, u32[]{:S(2)}) collective-permute-start(f32[1,64,512]{2,1,0:T(8,128)S(1)} %get-tuple-element.13), channel_id=1, source_target_pairs={{0,8},{8,16},{16,24},{24,32},{32,40},{40,48},{48,56},{56,64},{64,7... | collective-permute-start | bytes 393224 | tf_op jit(solution)/shard_map/ppermute | solution.py:18
  6.2 1.8 fusion.31
  8.0 3.2 %collective-permute-start.3 = (f32[64,1,512]{2,0,1:T(8,128)S(1)}, f32[64,1,512]{2,0,1:T(8,128)S(1)}, u32[]{:S(2)}, u32[]{:S(2)}) collective-permute-start(f32[64,1,512]{2,0,1:T(8,128)S(1)} %copy.49), channel_id=1, source_target_pairs={{0,1},{1,2},{2,3},{3,4},{4,5},{5,6},{6,7},{8,9},{9,10},{10,11},{11... | collective-permute-start | bytes 393224 | tf_op jit(solution)/shard_map/ppermute | solution.py:18
  11.2 1.3 collective-permute-start.2
  12.5 1.9 %collective-permute-start = (f32[1,64,512]{2,1,0:T(8,128)S(1)}, f32[1,64,512]{2,1,0:T(8,128)S(1)}, u32[]{:S(2)}, u32[]{:S(2)}) collective-permute-start(f32[1,64,512]{2,1,0:T(8,128)S(1)} %get-tuple-element.12), channel_id=1, source_target_pairs={{8,0},{16,8},{24,16},{32,24},{40,32},{48,40},{56,48},{64,56},{72,6... | collective-permute-start | bytes 393224 | tf_op jit(solution)/shard_map/ppermute | solution.py:19
  14.5 0.0 collective-permute-done.1
  14.5 0.0 slice-start
  14.5 0.7 constant_dynamic-update-slice_fusion.2
  15.2 0.0 slice-start.1
  15.2 8.8 %constant_dynamic-update-slice_fusion.1 = f32[66,64,512]{2,1,0:T(8,128)} fusion(f32[66,64,512]{2,1,0:T(8,128)} %constant_dynamic-update-slice_fusion.2, f32[64,64,512]{2,1,0:T(8,128)} %param.5), kind=kLoop, calls=%fused_computation.51 | loop fusion | bytes 16777216
  24.0 0.0 collective-permute-done.3
  24.0 0.1 copy.51
  24.1 0.0 collective-permute-done.2
  24.1 0.1 copy.50
  24.3 0.0 collective-permute-done
  24.3 0.7 constant_dynamic-update-slice_fusion
  24.9 0.0 slice-done
  24.9 0.0 slice-done.1
  24.9 20.7 %fusion.27 = (f32[64,64,512]{2,1,0:T(8,128)}, f32[64,64,512]{2,1,0:T(8,128)}) fusion(f32[64,64,512]{2,1,0:T(8,128)S(1)} %bitcast.21, f32[64,64,512]{2,1,0:T(8,128)} %param.6, f32[66,64,512]{2,1,0:T(8,128)} %constant_dynamic-update-slice_fusion, f32[64,1,512]{2,1,0:T(1,128)S(1)} %copy.51, f32[64,1,512]{2,1,0:T(1,128)S(1)} %copy.50, ...), kind=kLoop, calls=%fused_computation.53 | loop fusion | flops 50331648 | bytes 42729472 | tf_op jit(solution)/shard_map/add | solution.py:61
  45.7 1.0 fusion.30
  46.6 1.8 fusion.29
  48.5 4.0 %collective-permute-start.7 = (f32[64,1,512]{2,0,1:T(8,128)S(1)}, f32[64,1,512]{2,0,1:T(8,128)S(1)}, u32[]{:S(2)}, u32[]{:S(2)}) collective-permute-start(f32[64,1,512]{2,0,1:T(8,128)S(1)} %copy.38), channel_id=1, source_target_pairs={{0,1},{1,2},{2,3},{3,4},{4,5},{5,6},{6,7},{8,9},{9,10},{10,11},{11... | collective-permute-start | bytes 393224 | tf_op jit(solution)/shard_map/ppermute | solution.py:18
  52.5 1.3 collective-permute-start.6
  53.8 3.9 %collective-permute-start.5 = (f32[1,64,512]{2,1,0:T(8,128)S(1)}, f32[1,64,512]{2,1,0:T(8,128)S(1)}, u32[]{:S(2)}, u32[]{:S(2)}) collective-permute-start(f32[1,64,512]{2,1,0:T(8,128)S(1)} %get-tuple-element.8), channel_id=1, source_target_pairs={{0,8},{8,16},{16,24},{24,32},{32,40},{40,48},{48,56},{56,64},{64,7... | collective-permute-start | bytes 393224 | tf_op jit(solution)/shard_map/ppermute | solution.py:18
  57.7 2.1 %collective-permute-start.4 = (f32[1,64,512]{2,1,0:T(8,128)S(1)}, f32[1,64,512]{2,1,0:T(8,128)S(1)}, u32[]{:S(2)}, u32[]{:S(2)}) collective-permute-start(f32[1,64,512]{2,1,0:T(8,128)S(1)} %get-tuple-element.9), channel_id=1, source_target_pairs={{8,0},{16,8},{24,16},{32,24},{40,32},{48,40},{56,48},{64,56},{72,6... | collective-permute-start | bytes 393224 | tf_op jit(solution)/shard_map/ppermute | solution.py:19
  59.8 0.0 collective-permute-done.7
  59.8 0.1 copy.39
  60.0 0.0 collective-permute-done.6
  60.0 0.1 copy.37
  60.1 0.0 collective-permute-done.5
  60.1 3.9 %collective-permute-done.4 = f32[1,64,512]{2,1,0:T(8,128)S(1)} collective-permute-done((f32[1,64,512]{2,1,0:T(8,128)S(1)}, f32[1,64,512]{2,1,0:T(8,128)S(1)}, u32[]{:S(2)}, u32[]{:S(2)}) %collective-permute-start.4) | collective-permute-done | bytes 131104 | tf_op jit(solution)/shard_map/ppermute | solution.py:19
  64.0 39.2 %fusion.12 = f32[64,64,512]{2,1,0:T(8,128)} fusion(f32[64,64,512]{2,1,0:T(8,128)} %param.5, f32[64,64,512]{2,1,0:T(8,128)} %get-tuple-element.5, f32[64,64,512]{2,1,0:T(8,128)} %get-tuple-element.4, f32[64,1,512]{2,1,0:T(1,128)S(1)} %copy.39, f32[1,64,512]{2,1,0:T(8,128)S(1)} %collective-permute-done.4, f32[1,64,512]{2,1,0:T(8,128)S(1)} %collective-permute-done.5, ...), kind=kLoop, calls=%fused_computation.16 | loop fusion | flops 62914560 | bytes 42467328 | tf_op jit(solution)/shard_map/add | solution.py:63
  103.2 0.0 copy-done
  103.2 0.0 copy-start.2
  103.2 4.6 %fusion.21 = f32[64,64,128]{2,1,0:T(8,128)S(1)} fusion(f32[64,64,512]{2,1,0:T(8,128)} %fusion.12, bf16[512,128]{1,0:T(8,128)(2,1)S(1)} %copy-done), kind=kOutput, calls=%fused_computation.41 | convolution fusion | flops 538968064 | bytes 10616832 | tf_op jit(solution)/shard_map/dot_general | solution.py:65
  107.8 0.0 copy-done.2
  107.9 0.0 copy-start.1
  107.9 2.0 %convolution_bitcast_fusion = f32[64,8,8,128]{3,2,1,0:T(8,128)S(1)} fusion(f32[64,64,128]{2,1,0:T(8,128)S(1)} %fusion.21, f32[64,64]{1,0:T(8,128)S(1)} %copy-done.2), kind=kOutput, calls=%fused_computation.44 | convolution fusion | flops 402653184 | bytes 4210688 | tf_op jit(solution)/shard_map/xyc,yb->xbc/dot_general | solution.py:68
  109.9 0.1 copy.55
  110.0 39.4 %all_to_all.10 = f32[8,64,8,128]{3,2,1,0:T(8,128)S(1)} all-to-all(f32[8,64,8,128]{3,2,1,0:T(8,128)S(1)} %bitcast.22), channel_id=1, replica_groups=mesh['gx'=16,'gy'=8] {'gy'}, dimensions={0} | all-to-all | bytes 4194304 | tf_op jit(solution)/shard_map/all_to_all | solution.py:37
  149.4 0.1 reduce_sum.18
  149.5 0.0 copy-done.1
  149.5 1.8 convolution_bitcast_fusion.1
  151.4 1.9 copy.44
  153.2 33.8 %all_to_all.11 = f32[16,32,8,128]{3,2,1,0:T(8,128)S(1)} all-to-all(f32[16,32,8,128]{3,2,1,0:T(8,128)} %bitcast.23), channel_id=1, replica_groups=mesh['gx'=16,'gy'=8] {'gx'}, dimensions={0} | all-to-all | bytes 4194304 | tf_op jit(solution)/shard_map/all_to_all | solution.py:37
  187.0 0.8 reduce_sum.19
  (5 shorter events, 0.0 us)
Async XLA Ops:
  0.6 102.6 %copy-start = (bf16[512,128]{1,0:T(8,128)(2,1)S(1)}, bf16[512,128]{1,0:T(8,128)(2,1)}, u32[]{:S(2)}) copy-start(bf16[512,128]{1,0:T(8,128)(2,1)} %param.9) | copy-start | bytes 393220
  1.7 12.8 %collective-permute-start.1 = (f32[1,64,512]{2,1,0:T(8,128)S(1)}, f32[1,64,512]{2,1,0:T(8,128)S(1)}, u32[]{:S(2)}, u32[]{:S(2)}) collective-permute-start(f32[1,64,512]{2,1,0:T(8,128)S(1)} %get-tuple-element.13), channel_id=1, source_target_pairs={{0,8},{8,16},{16,24},{24,32},{32,40},{40,48},{48,56},{56,64},{64,7... | collective-permute-start | bytes 393224 | tf_op jit(solution)/shard_map/ppermute | solution.py:18
  8.0 16.0 %collective-permute-start.3 = (f32[64,1,512]{2,0,1:T(8,128)S(1)}, f32[64,1,512]{2,0,1:T(8,128)S(1)}, u32[]{:S(2)}, u32[]{:S(2)}) collective-permute-start(f32[64,1,512]{2,0,1:T(8,128)S(1)} %copy.49), channel_id=1, source_target_pairs={{0,1},{1,2},{2,3},{3,4},{4,5},{5,6},{6,7},{8,9},{9,10},{10,11},{11... | collective-permute-start | bytes 393224 | tf_op jit(solution)/shard_map/ppermute | solution.py:18
  11.2 12.9 %collective-permute-start.2 = (f32[64,1,512]{2,0,1:T(8,128)S(1)}, f32[64,1,512]{2,0,1:T(8,128)S(1)}, u32[]{:S(2)}, u32[]{:S(2)}) collective-permute-start(f32[64,1,512]{2,0,1:T(8,128)S(1)} %copy.48), channel_id=1, source_target_pairs={{1,0},{2,1},{3,2},{4,3},{5,4},{6,5},{7,6},{9,8},{10,9},{11,10},{12... | collective-permute-start | bytes 393224 | tf_op jit(solution)/shard_map/ppermute | solution.py:19
  12.5 11.7 %collective-permute-start = (f32[1,64,512]{2,1,0:T(8,128)S(1)}, f32[1,64,512]{2,1,0:T(8,128)S(1)}, u32[]{:S(2)}, u32[]{:S(2)}) collective-permute-start(f32[1,64,512]{2,1,0:T(8,128)S(1)} %get-tuple-element.12), channel_id=1, source_target_pairs={{8,0},{16,8},{24,16},{32,24},{40,32},{48,40},{56,48},{64,56},{72,6... | collective-permute-start | bytes 393224 | tf_op jit(solution)/shard_map/ppermute | solution.py:19
  14.5 10.5 %slice-start = ((s8[8388608]{0:T(1024)(128)(4,1)}), s8[4194304]{0:T(1024)(128)(4,1)S(1)}, s32[]{:S(2)}) async-start(s8[8388608]{0:T(1024)(128)(4,1)} %bitcast.20), calls=%async_computation.2 | async-start | bytes 8388608
  15.2 9.8 %slice-start.1 = ((s8[8388608]{0:T(1024)(128)(4,1)}), s8[4194304]{0:T(1024)(128)(4,1)S(1)}, s32[]{:S(2)}) async-start(s8[8388608]{0:T(1024)(128)(4,1)} %bitcast.20), calls=%async_computation.3 | async-start | bytes 8388608
  48.5 11.3 %collective-permute-start.7 = (f32[64,1,512]{2,0,1:T(8,128)S(1)}, f32[64,1,512]{2,0,1:T(8,128)S(1)}, u32[]{:S(2)}, u32[]{:S(2)}) collective-permute-start(f32[64,1,512]{2,0,1:T(8,128)S(1)} %copy.38), channel_id=1, source_target_pairs={{0,1},{1,2},{2,3},{3,4},{4,5},{5,6},{6,7},{8,9},{9,10},{10,11},{11... | collective-permute-start | bytes 393224 | tf_op jit(solution)/shard_map/ppermute | solution.py:18
  52.5 7.5 %collective-permute-start.6 = (f32[64,1,512]{2,0,1:T(8,128)S(1)}, f32[64,1,512]{2,0,1:T(8,128)S(1)}, u32[]{:S(2)}, u32[]{:S(2)}) collective-permute-start(f32[64,1,512]{2,0,1:T(8,128)S(1)} %copy.36), channel_id=1, source_target_pairs={{1,0},{2,1},{3,2},{4,3},{5,4},{6,5},{7,6},{9,8},{10,9},{11,10},{12... | collective-permute-start | bytes 393224 | tf_op jit(solution)/shard_map/ppermute | solution.py:19
  53.8 6.4 %collective-permute-start.5 = (f32[1,64,512]{2,1,0:T(8,128)S(1)}, f32[1,64,512]{2,1,0:T(8,128)S(1)}, u32[]{:S(2)}, u32[]{:S(2)}) collective-permute-start(f32[1,64,512]{2,1,0:T(8,128)S(1)} %get-tuple-element.8), channel_id=1, source_target_pairs={{0,8},{8,16},{16,24},{24,32},{32,40},{40,48},{48,56},{56,64},{64,7... | collective-permute-start | bytes 393224 | tf_op jit(solution)/shard_map/ppermute | solution.py:18
  57.7 6.3 %collective-permute-start.4 = (f32[1,64,512]{2,1,0:T(8,128)S(1)}, f32[1,64,512]{2,1,0:T(8,128)S(1)}, u32[]{:S(2)}, u32[]{:S(2)}) collective-permute-start(f32[1,64,512]{2,1,0:T(8,128)S(1)} %get-tuple-element.9), channel_id=1, source_target_pairs={{8,0},{16,8},{24,16},{32,24},{40,32},{48,40},{56,48},{64,56},{72,6... | collective-permute-start | bytes 393224 | tf_op jit(solution)/shard_map/ppermute | solution.py:19
  103.2 4.7 %copy-start.2 = (f32[64,64]{1,0:T(8,128)S(1)}, f32[64,64]{1,0:T(8,128)}, u32[]{:S(2)}) copy-start(f32[64,64]{1,0:T(8,128)} %param.8) | copy-start | bytes 49156
  107.9 41.7 %copy-start.1 = (f32[64,512]{1,0:T(8,128)S(1)}, f32[64,512]{1,0:T(8,128)}, u32[]{:S(2)}) copy-start(f32[64,512]{1,0:T(8,128)} %param.7) | copy-start | bytes 393220
where the time goes:
time: 188 us
  blocking collectives  73.2 us (39%)
  other arithmetic  60.8 us (32%)
  starting transfers between devices  22.2 us (12%)
  local copies, waits for them, and re-layouts  18.3 us (10%)
  matrix products  8.49 us (5%)
  waiting for transfers between devices  3.88 us (2%)
    all_to_all x2, blocking collectives, sent_and_summed(): lax.all_to_all(in_blocks(array, dim, peers), axis, 0, 0, tiled=True)  73.2 us
    add x1, other arithmetic, on_device(): advanced = scalar + 0.5 * (first + second)  39.2 us
    add x1, other arithmetic, on_device(): middle = scalar + first  20.7 us
    ppermute x4, starting transfers between devices, extended(): lax.ppermute(last, axis, up)  15.6 us
    unnamed x16, local copies, waits for them, and re-layouts  9.8 us
    ppermute x4, starting transfers between devices, extended(): lax.ppermute(first, axis, [(b, a) for a, b in up])  6.61 us
    dot_general x1, matrix products, on_device(): jnp.dot(lowered.reshape(cells_x * cells_y, depth), factor_z, preferred_el...  4.64 us
    slice x4, local copies, waits for them, and re-layouts, extended(): first = lax.slice_in_dim(array, 0, width, axis=dim)  4.62 us
  transfers between devices with their start and end apart: 8, of which 1 were waited for; matrix products, arithmetic and copies ran while one was open for 6% of the time, Pallas kernels for 0%

commit v1 on v0

v1 whole, which is shorter than its diff:
```python
import jax
import jax.numpy as jnp
from jax import lax
from jax.experimental import pallas as pl
from jax.experimental.pallas import tpu as pltpu
from jax.sharding import PartitionSpec as P

MESH = pl.DeviceIdType.MESH
spread_rate = 0.12
activation = 2.0
PLANES, ROWS, LANES, PARTS = 64, 64, 128, 4
CHUNK = 8
CHUNKS = PLANES // CHUNK
TOP = 8
BAND = 16


def split(value):
    high = value.astype(jnp.bfloat16)
    low = (value - high.astype(jnp.float32)).astype(jnp.bfloat16)
    return high, low


def kernel(
    scalar, prefactor, factor_x, factor_y, factor_z, advanced, core_out,
    field, middle, pref, lowered, fz, fy, fx_all, fy_t, fx_t,
    faces_s, halo_s, faces_m, halo_m,
    y_red, y_in1, y_in2, z_in, gathered, x_out, x_in,
    load_sem, pref_sem, small_sem,
    fs_send, fs_recv, fm_send, fm_recv, xs_send, xs_recv, xm_send, xm_recv,
    fx_send, fx_recv, y1_send, y1_recv, y2_send, y2_recv, z_send, z_recv, c_send, c_recv, xr_send, xr_recv,
):
    gx, gy = lax.axis_index("gx"), lax.axis_index("gy")
    core, x, zl = gx % 2, (gx // 2) % 4, gx // 8
    y, zh = gy % 4, gy // 4

    def device(core, x, zl, y, zh):
        return (zl * 8 + x * 2 + core, zh * 4 + y)

    up_x, down_x = ((gx + 1) % 16, gy), ((gx + 15) % 16, gy)
    up_y, down_y = (gx, (gy + 1) % 8), (gx, (gy + 7) % 8)
    y_by1 = y + 1 - 2 * (y % 2)
    y_by3 = 3 - y
    pair_a, pair_b = device(core, x, zl, y_by1, zh), device(core, x, zl, y_by3, zh)
    z_peers = [device(core, x, 1 - zl, y, zh), device(core, x, zl, y, 1 - zh), device(core, x, 1 - zl, y, 1 - zh)]
    partner = device(1 - core, x, zl, y, zh)
    fx_peers = [partner, z_peers[0], device(1 - core, x, 1 - zl, y, zh)]
    x_peers = [device(core, (x + j) % 4, zl, y, zh) for j in (1, 2, 3)]

    def load(k, part):
        return pltpu.make_async_copy(
            scalar.at[pl.ds(k * CHUNK, CHUNK), :, pl.ds(part * LANES, LANES)],
            field.at[pl.ds(k * CHUNK + 1, CHUNK), part, pl.ds(TOP, ROWS), :],
            load_sem.at[k, part],
        )

    def load_pref(k):
        rows = pl.ds(k * CHUNK, CHUNK)
        return pltpu.make_async_copy(prefactor.at[rows], pref.at[rows], pref_sem.at[k])

    for k in [7, 0, 6, 1, 2, 3, 4, 5]:
        for part in range(PARTS):
            load(k, part).start()
    fx_load = pltpu.make_async_copy(factor_x, fx_all.at[core, zl], small_sem.at[0])
    fz_load = pltpu.make_async_copy(factor_z, fz, small_sem.at[1])
    fy_load = pltpu.make_async_copy(factor_y, fy, small_sem.at[2])
    fx_load.start()
    for k in [7, 0, 1]:
        load_pref(k).start()
    fz_load.start()
    fy_load.start()
    for k in [2, 3, 4, 5, 6]:
        load_pref(k).start()

    barrier = pltpu.get_barrier_semaphore()
    peers = [up_x, down_x, up_y, down_y, pair_a, pair_b, *z_peers, partner, fx_peers[2], *x_peers]
    for peer in peers:
        pl.semaphore_signal(barrier, inc=1, device_id=peer, device_id_type=MESH)
    pl.semaphore_wait(barrier, len(peers))

    def remote(src, dst, send, recv, to):
        return pltpu.make_async_remote_copy(
            src_ref=src, dst_ref=dst, send_sem=send, recv_sem=recv, device_id=to, device_id_type=MESH
        )

    def plane_of(buffer, index):
        return buffer.at[index, :, pl.ds(TOP, ROWS), :]

    def x_faces(buffer, send, recv):
        low = remote(plane_of(buffer, 1), plane_of(buffer, PLANES + 1), send.at[0], recv.at[0], down_x)
        high = remote(plane_of(buffer, PLANES), plane_of(buffer, 0), send.at[1], recv.at[1], up_x)
        return low, high

    def y_faces(faces, halo, send, recv, k):
        rows = pl.ds(k * CHUNK * PARTS, CHUNK * PARTS)
        low = remote(faces.at[0, rows], halo.at[1, rows], send.at[0, k], recv.at[0, k], down_y)
        high = remote(faces.at[1, rows], halo.at[0, rows], send.at[1, k], recv.at[1, k], up_y)
        return low, high

    s_low, s_high = x_faces(field, xs_send, xs_recv)
    m_low, m_high = x_faces(middle, xm_send, xm_recv)

    def send_faces(k):
        for part in range(PARTS):
            load(k, part).wait()
        for i in range(CHUNK):
            for part in range(PARTS):
                at = pl.ds((k * CHUNK + i) * PARTS + part, 1)
                faces_s[0, at, :] = field[k * CHUNK + i + 1, part, TOP : TOP + 1, :]
                faces_s[1, at, :] = field[k * CHUNK + i + 1, part, TOP + ROWS - 1 : TOP + ROWS, :]
        for copy in y_faces(faces_s, halo_s, fs_send, fs_recv, k):
            copy.start()

    send_faces(7)
    s_high.start()
    send_faces(0)
    s_low.start()
    send_faces(6)

    def rest(k, carry):
        send_faces(k)
        return carry

    lax.fori_loop(1, 6, rest, 0)

    fx_copies = [
        remote(fx_all.at[core, zl], fx_all.at[core, zl], fx_send.at[i], fx_recv.at[i], to)
        for i, to in enumerate(fx_peers)
    ]
    fx_load.wait()
    for copy in fx_copies:
        copy.start()
    fz_load.wait()
    fy_load.wait()
    eye = (
        lax.broadcasted_iota(jnp.int32, (64, 64), 0) == lax.broadcasted_iota(jnp.int32, (64, 64), 1)
    ).astype(jnp.bfloat16)
    turned = (((1,), (1,)), ((), ()))
    fy_high, fy_low = (
        lax.dot_general(eye, part, turned, preferred_element_type=jnp.float32).astype(jnp.bfloat16)
        for part in split(fy[...])
    )
    fy_t[...] = jnp.concatenate([fy_high, fy_high, fy_low], axis=1)

    lane = lax.broadcasted_iota(jnp.int32, (BAND, LANES), 1)
    at_left, at_right = lane == 0, lane == LANES - 1

    def fill_halo(buffer, halo, plane):
        for part in range(PARTS):
            at = pl.ds(plane * PARTS + part, 1)
            buffer[plane + 1, part, TOP - 1 : TOP, :] = jnp.where(gy > 0, halo[0, at, :], 0.0)
            buffer[plane + 1, part, TOP + ROWS : TOP + ROWS + 1, :] = jnp.where(gy < 7, halo[1, at, :], 0.0)

    def stepped(buffer, plane, row):
        at = plane + 1
        own = slice(TOP + row, TOP + row + BAND)
        centers = [buffer[at, part, own, :] for part in range(PARTS)]
        lefts = [pltpu.roll(c, 1, 1) for c in centers]
        rights = [pltpu.roll(c, LANES - 1, 1) for c in centers]
        results = []
        for part, c in enumerate(centers):
            left = jnp.where(at_left, lefts[part - 1] if part > 0 else 0.0, lefts[part])
            right = jnp.where(at_right, rights[part + 1] if part + 1 < PARTS else 0.0, rights[part])
            beside = buffer[at + 1, part, own, :] + buffer[at - 1, part, own, :]
            beside = beside + (
                buffer[at, part, TOP + row + 1 : TOP + row + 1 + BAND, :]
                + buffer[at, part, TOP + row - 1 : TOP + row - 1 + BAND, :]
            )
            beside = beside + (left + right)
            factor = pref[plane, row : row + BAND, part * LANES : (part + 1) * LANES]
            source = factor * jnp.exp(-activation / (1.0 + c * c))
            results.append((1.0 - 6.0 * spread_rate) * c + spread_rate * beside + source)
        return results

    def clear_plane(buffer, index):
        for part in range(PARTS):
            buffer[index, part, TOP : TOP + ROWS, :] = jnp.zeros((ROWS, LANES), jnp.float32)

    def first_stage(k):
        load_pref(k).wait()
        low, high = y_faces(faces_s, halo_s, fs_send, fs_recv, k)
        low.wait_recv()
        high.wait_recv()

        @pl.when(k == CHUNKS - 1)
        def _():
            s_low.wait_recv()

            @pl.when(gx == 15)
            def _():
                clear_plane(field, PLANES + 1)

        @pl.when(k == 0)
        def _():
            s_high.wait_recv()

            @pl.when(gx == 0)
            def _():
                clear_plane(field, 0)

        def plane_step(i, carry):
            plane = k * CHUNK + i
            fill_halo(field, halo_s, plane)
            for row in range(0, ROWS, BAND):
                for part, value in enumerate(stepped(field, plane, row)):
                    middle[plane + 1, part, TOP + row : TOP + row + BAND, :] = value
                    at = pl.ds(plane * PARTS + part, 1)
                    if row == 0:
                        faces_m[0, at, :] = value[0:1, :]
                    if row == ROWS - BAND:
                        faces_m[1, at, :] = value[BAND - 1 : BAND, :]
            return carry

        lax.fori_loop(0, CHUNK, plane_step, 0)
        for copy in y_faces(faces_m, halo_m, fm_send, fm_recv, k):
            copy.start()

        @pl.when(k == CHUNKS - 1)
        def _():
            m_high.start()

        @pl.when(k == 0)
        def _():
            m_low.start()

    def y_first(k):
        a = remote(y_red.at[k, pl.ds(1, 2), :, pl.ds(0, 4)], y_in1.at[k, 0], y1_send.at[k, 0], y1_recv.at[k, 0], pair_a)
        b = remote(y_red.at[k, pl.ds(2, 2), :, pl.ds(4, 4)], y_in1.at[k, 1], y1_send.at[k, 1], y1_recv.at[k, 1], pair_b)
        return a, b

    def y_second(k):
        a = remote(y_red.at[k, 3, :, pl.ds(0, 4)], y_in2.at[k, 0], y2_send.at[k, 0], y2_recv.at[k, 0], pair_b)
        b = remote(y_red.at[k, 1, :, pl.ds(4, 4)], y_in2.at[k, 1], y2_send.at[k, 1], y2_recv.at[k, 1], pair_a)
        return a, b

    def z_copies(k):
        return [
            remote(y_red.at[k, 0, block], z_in.at[k, i], z_send.at[k, i], z_recv.at[k, i], z_peers[i])
            for i, block in enumerate((zh, 1 - zh, 1 - zh))
        ]

    def core_copy(k):
        block = gathered.at[core, :, pl.ds(k * CHUNK, CHUNK)]
        return remote(block, block, c_send.at[k], c_recv.at[k], partner)

    def second_stage(k):
        low, high = y_faces(faces_m, halo_m, fm_send, fm_recv, k)
        low.wait_recv()
        high.wait_recv()

        @pl.when(k == CHUNKS - 1)
        def _():
            m_low.wait_recv()

            @pl.when(gx == 15)
            def _():
                clear_plane(middle, PLANES + 1)

        @pl.when(k == 0)
        def _():
            m_high.wait_recv()

            @pl.when(gx == 0)
            def _():
                clear_plane(middle, 0)

        def plane_step(i, carry):
            plane = k * CHUNK + i
            fill_halo(middle, halo_m, plane)
            for row in range(0, ROWS, BAND):
                for part, value in enumerate(stepped(middle, plane, row)):
                    value = 0.5 * (field[plane + 1, part, TOP + row : TOP + row + BAND, :] + value)
                    lanes = slice(part * LANES, (part + 1) * LANES)
                    advanced[plane, row : row + BAND, lanes] = value
                    lowered[i, row : row + BAND, lanes] = value.astype(jnp.bfloat16)
            return carry

        lax.fori_loop(0, CHUNK, plane_step, 0)
        z_red = jnp.dot(
            lowered[...].reshape(CHUNK * ROWS, PARTS * LANES), fz[...], preferred_element_type=jnp.float32
        )
        blocks = [y, y_by1, (y + 2) % 4, y_by3]
        for i in range(0, CHUNK, 2):
            pair = jnp.concatenate([z_red[i * ROWS : (i + 1) * ROWS], z_red[(i + 1) * ROWS : (i + 2) * ROWS]], axis=1)
            high, low = split(pair)
            stacked = jnp.concatenate([high, low, high], axis=0)
            both = jnp.dot(fy_t[...], stacked, preferred_element_type=jnp.float32)
            for owner in range(8):
                for j in range(2):
                    y_red[k, blocks[owner % 4], owner // 4, i + j] = both[
                        owner * 8 : owner * 8 + 8, j * LANES : (j + 1) * LANES
                    ]
        for copy in y_first(k):
            copy.start()

    def y_first_done(k):
        for copy in y_first(k):
            copy.wait_recv()
        y_red[k, 0, :, 0:4] += y_in1[k, 0, 0]
        y_red[k, 3, :, 0:4] += y_in1[k, 0, 1]
        y_red[k, 1, :, 4:8] += y_in1[k, 1, 0]
        y_red[k, 0, :, 4:8] += y_in1[k, 1, 1]
        for copy in y_second(k):
            copy.start()

    def y_second_done(k):
        for copy in y_second(k):
            copy.wait_recv()
        y_red[k, 0, :, 0:4] += y_in2[k, 0]
        y_red[k, 0, :, 4:8] += y_in2[k, 1]
        for copy in z_copies(k):
            copy.start()

    def z_done(k):
        for copy in z_copies(k):
            copy.wait_recv()
        rows = pl.ds(k * CHUNK, CHUNK)
        gathered[core, zl, rows] = y_red[k, 0, zh] + z_in[k, 1]
        gathered[core, 1 - zl, rows] = z_in[k, 0] + z_in[k, 2]
        core_copy(k).start()

    def prepare_x():
        for copy in fx_copies:
            copy.wait_recv()
        entry = lax.broadcasted_iota(jnp.int32, (128, 512), 0)
        wanted = zl * 256 + (entry // 32) * 64 + core * 32 + entry % 32
        picked = (lax.broadcasted_iota(jnp.int32, (128, 512), 1) == wanted).astype(jnp.bfloat16)
        high, low = (
            lax.dot_general(picked, part, turned, preferred_element_type=jnp.float32).astype(jnp.bfloat16)
            for part in split(fx_all[...].reshape(256, 512))
        )
        fx_t[...] = jnp.concatenate([high, high, low], axis=1)

    def step(t, carry):
        pl.when(t < CHUNKS)(lambda: first_stage((t + CHUNKS - 1) % CHUNKS))
        pl.when((t >= 2) & (t < CHUNKS + 2))(lambda: second_stage(t - 2))
        pl.when(t == CHUNKS + 1)(prepare_x)
        pl.when((t >= 4) & (t < CHUNKS + 4))(lambda: y_first_done(t - 4))
        pl.when((t >= 6) & (t < CHUNKS + 6))(lambda: y_second_done(t - 6))
        pl.when(t >= 8)(lambda: z_done(t - 8))
        return carry

    lax.fori_loop(0, CHUNKS + 8, step, 0)

    for k in range(CHUNKS):
        core_copy(k).wait_recv()
    for b in range(0, 8, 2):
        pair = jnp.concatenate(
            [gathered[:, :, :, b + j, :].reshape(256, LANES) for j in range(2)], axis=1
        )
        high, low = split(pair)
        stacked = jnp.concatenate([high, low, high], axis=0)
        both = jnp.dot(fx_t[...], stacked, preferred_element_type=jnp.float32)
        for owner in range(4):
            for j in range(2):
                x_out[owner, b + j] = both[owner * 32 : owner * 32 + 32, j * LANES : (j + 1) * LANES]
    x_copies = [
        remote(x_out.at[(x + 1 + i) % 4], x_in.at[i], xr_send.at[i], xr_recv.at[i], to) for i, to in enumerate(x_peers)
    ]
    for copy in x_copies:
        copy.start()
    for copy in x_copies:
        copy.wait_recv()
    for b in range(8):
        core_out[:, b, :] = (x_out[x, b] + x_in[0, b]) + (x_in[1, b] + x_in[2, b])

    for copy in (s_low, s_high, m_low, m_high, *fx_copies, *x_copies):
        copy.wait_send()

    def drain(k, carry):
        for copy in (
            *y_faces(faces_s, halo_s, fs_send, fs_recv, k),
            *y_faces(faces_m, halo_m, fm_send, fm_recv, k),
            *y_first(k), *y_second(k), *z_copies(k), core_copy(k),
        ):
            copy.wait_send()
        return carry

    lax.fori_loop(0, CHUNKS, drain, 0)


def on_device(scalar, prefactor, factor_x, factor_y, factor_z):
    f32, bf16 = jnp.float32, jnp.bfloat16
    dma = pltpu.SemaphoreType.DMA
    vmem = pltpu.VMEM
    padded = vmem((PLANES + 2, PARTS, ROWS + 16, LANES), f32)
    faces = vmem((2, PLANES * PARTS, LANES), f32)
    anywhere = pl.BlockSpec(memory_space=pl.ANY)
    return pl.pallas_call(
        kernel,
        out_shape=(
            jax.ShapeDtypeStruct((PLANES, ROWS, PARTS * LANES), f32),
            jax.ShapeDtypeStruct((32, 8, LANES), f32),
        ),
        in_specs=[anywhere] * 5,
        out_specs=(pl.BlockSpec(memory_space=vmem), pl.BlockSpec(memory_space=vmem)),
        scratch_shapes=[
            padded, padded, vmem((PLANES, ROWS, PARTS * LANES), f32), vmem((CHUNK, ROWS, PARTS * LANES), bf16),
            vmem((512, 128), bf16), vmem((64, 64), f32), vmem((2, 2, 64, 512), f32),
            vmem((64, 192), bf16), vmem((128, 768), bf16),
            faces, faces, faces, faces,
            vmem((CHUNKS, 4, 2, CHUNK, 8, LANES), f32), vmem((CHUNKS, 2, 2, 2, 4, 8, LANES), f32),
            vmem((CHUNKS, 2, 2, 4, 8, LANES), f32), vmem((CHUNKS, 3, CHUNK, 8, LANES), f32),
            vmem((2, 2, PLANES, 8, LANES), f32), vmem((4, 8, 32, LANES), f32), vmem((3, 8, 32, LANES), f32),
            dma((CHUNKS, PARTS)), dma((CHUNKS,)), dma((3,)),
            dma((2, CHUNKS)), dma((2, CHUNKS)), dma((2, CHUNKS)), dma((2, CHUNKS)),
            dma((2,)), dma((2,)), dma((2,)), dma((2,)),
            dma((3,)), dma((3,)), dma((CHUNKS, 2)), dma((CHUNKS, 2)), dma((CHUNKS, 2)), dma((CHUNKS, 2)),
            dma((CHUNKS, 3)), dma((CHUNKS, 3)), dma((CHUNKS,)), dma((CHUNKS,)), dma((3,)), dma((3,)),
        ],
        compiler_params=pltpu.CompilerParams(collective_id=0, has_side_effects=True, vmem_limit_bytes=50 << 20),
        name="heun_tucker",
    )(scalar, prefactor, factor_x, factor_y, factor_z)


def solution(mesh):
    return jax.shard_map(
        on_device,
        mesh=mesh,
        in_specs=(P("gx", "gy", None), P("gx", "gy", None), P("gx", None), P("gy", None), P()),
        out_specs=(P("gx", "gy", None), P("gx", "gy", None)),
        check_vma=False,
    )
```

time: 188 us -> 87.1 us (0.46)
  Pallas kernels: 0 us -> 74.4 us
  blocking collectives: 73.2 us -> 0 us
  other arithmetic: 60.8 us -> 0 us
  starting transfers between devices: 22.2 us -> 0 us
  matrix products: 8.49 us -> 0 us
  local copies, waits for them, and re-layouts: 18.3 us -> 11.8 us
  waiting for transfers between devices: 3.88 us -> 0 us
    pallas_call x0 -> x1, Pallas kernels: none -> 74.4 us  [on_device(): pl.pallas_call(kernel, out_shape=(jax.ShapeDtypeStruct((PLANES, ROWS, PAR...]
    all_to_all x2 -> x0, blocking collectives: 73.2 us -> none  [sent_and_summed(): lax.all_to_all(in_blocks(array, dim, peers), axis, 0, 0, tiled=True)]
    add x2 -> x0, other arithmetic: 59.9 us -> none  [the longest x1 39.2 us: on_device(): advanced = scalar + 0.5 * (first + second)]
    ppermute x8 -> x0, starting transfers between devices: 22.2 us -> none  [the longest x4 15.6 us: extended(): lax.ppermute(last, axis, up)]
    dot_general x3 -> x0, matrix products: 8.49 us -> none  [the longest x1 4.64 us: on_device(): jnp.dot(lowered.reshape(cells_x * cells_y, depth), factor_z, preferred_el...]
    slice x6 -> x0, local copies, waits for them, and re-layouts: 5.62 us -> none  [the longest x4 4.62 us: extended(): first = lax.slice_in_dim(array, 0, width, axis=dim)]
    ppermute x8 -> x0, waiting for transfers between devices: 3.88 us -> none  [the longest x4 3.87 us: extended(): lax.ppermute(first, axis, [(b, a) for a, b in up])]
    unnamed x16 -> x8, local copies, waits for them, and re-layouts: 9.8 us -> 11.8 us
  transfers between devices with their start and end apart: 8 -> 0, of which waited for: 1 -> 0; matrix products, arithmetic and copies ran while one was open for 6% -> 0% of each run, Pallas kernels for 0% -> 0%
where the time goes in v1:
time: 87.1 us; the launch traced here: 86.9 us
  Pallas kernels  74.4 us (85%)
  local copies, waits for them, and re-layouts  11.8 us (14%)
    pallas_call x1, Pallas kernels, on_device(): pl.pallas_call(kernel, out_shape=(jax.ShapeDtypeStruct((PLANES, ROWS, PAR...  74.4 us
    unnamed x8, local copies, waits for them, and re-layouts  11.8 us

profile of v1, /device:TPU:1, one launch (start us, length us, event | category | flops | bytes accessed | tf_op | source)
XLA Modules:
  0.0 86.9 jit_solution(14298621545939271379)
XLA Ops:
  0.6 0.0 copy-start
  0.6 0.9 %copy-done = f32[64,512]{1,0:T(8,128)S(1)} copy-done((f32[64,512]{1,0:T(8,128)S(1)}, f32[64,512]{1,0:T(8,128)}, u32[]{:S(2)}) %copy-start) | copy-done | bytes 131096
  1.5 0.0 copy-start.1
  1.5 0.9 %copy-done.1 = bf16[512,128]{1,0:T(8,128)(2,1)S(1)} copy-done((bf16[512,128]{1,0:T(8,128)(2,1)S(1)}, bf16[512,128]{1,0:T(8,128)(2,1)}, u32[]{:S(2)}) %copy-start.1) | copy-done | bytes 131096
  2.4 0.0 copy-start.2
  2.4 0.8 copy-done.2
  3.2 74.4 %heun_tucker.1 = (f32[64,64,512]{2,1,0:T(8,128)}, f32[32,8,128]{2,1,0:T(8,128)S(1)}) custom-call(f32[64,64,512]{2,1,0:T(8,128)} %scalar.1, f32[64,64,512]{2,1,0:T(8,128)} %prefactor.1, f32[64,512]{1,0:T(8,128)S(1)} %copy-done, f32[64,64]{1,0:T(8,128)S(1)} %copy-done.2, bf16[512,128]{1,0:T(8,128)(2,1)S(1)} %copy-done.1), custom_call_target="tpu_custom_call" | custom-call | tf_op jit(solution)/shard_map/heun_tucker/pallas_call | solution.py:389
  77.6 8.6 %copy.9 = f32[64,64,512]{2,1,0:T(8,128)} copy(f32[64,64,512]{2,1,0:T(8,128)} %get-tuple-element.4) | data formatting | bytes 16777216
  86.2 0.7 copy.10
Async XLA Ops:
  0.6 0.9 %copy-start = (f32[64,512]{1,0:T(8,128)S(1)}, f32[64,512]{1,0:T(8,128)}, u32[]{:S(2)}) copy-start(f32[64,512]{1,0:T(8,128)} %factor_x.1) | copy-start | bytes 393220
  1.5 0.9 %copy-start.1 = (bf16[512,128]{1,0:T(8,128)(2,1)S(1)}, bf16[512,128]{1,0:T(8,128)(2,1)}, u32[]{:S(2)}) copy-start(bf16[512,128]{1,0:T(8,128)(2,1)} %factor_z.1) | copy-start | bytes 393220
  2.4 0.8 copy-start.2

commit v2 on v1

--- a/solution.py
+++ b/solution.py
@@ -12,7 +12,12 @@
 CHUNK = 8
 CHUNKS = PLANES // CHUNK
 TOP = 8
+PADDED = ROWS + 16
+STRIP = CHUNK * PARTS
 BAND = 16
+FIX = 4
+SECOND = 8
+FIRST_SUM, SECOND_SUM, Z_SUM = SECOND + 2, SECOND + 4, SECOND + 6
 
 
 def split(value):
@@ -23,7 +28,7 @@
 
 def kernel(
     scalar, prefactor, factor_x, factor_y, factor_z, advanced, core_out,
-    field, middle, pref, lowered, fz, fy, fx_all, fy_t, fx_t,
+    field, middle, pref, beside_x, lowered, fz, fy, fx_all, fy_t, fx_t,
     faces_s, halo_s, faces_m, halo_m,
     y_red, y_in1, y_in2, z_in, gathered, x_out, x_in,
     load_sem, pref_sem, small_sem,
@@ -58,24 +63,47 @@
         rows = pl.ds(k * CHUNK, CHUNK)
         return pltpu.make_async_copy(prefactor.at[rows], pref.at[rows], pref_sem.at[k])
 
-    for k in [7, 0, 6, 1, 2, 3, 4, 5]:
+    for part in range(PARTS):
+        load(7, part).start()
+        load(6, part).start()
+    load_pref(7).start()
+    for k in (0, 1):
         for part in range(PARTS):
             load(k, part).start()
+    load_pref(0).start()
     fx_load = pltpu.make_async_copy(factor_x, fx_all.at[core, zl], small_sem.at[0])
     fz_load = pltpu.make_async_copy(factor_z, fz, small_sem.at[1])
     fy_load = pltpu.make_async_copy(factor_y, fy, small_sem.at[2])
-    fx_load.start()
-    for k in [7, 0, 1]:
-        load_pref(k).start()
-    fz_load.start()
-    fy_load.start()
-    for k in [2, 3, 4, 5, 6]:
-        load_pref(k).start()
+    for k in range(2, CHUNKS - 2):
+        for part in range(PARTS):
+            load(k, part).start()
+        load_pref(k - 1).start()
+        if k == 2:
+            fx_load.start()
+            fz_load.start()
+            fy_load.start()
+    load_pref(5).start()
+    load_pref(6).start()
 
     barrier = pltpu.get_barrier_semaphore()
     peers = [up_x, down_x, up_y, down_y, pair_a, pair_b, *z_peers, partner, fx_peers[2], *x_peers]
     for peer in peers:
         pl.semaphore_signal(barrier, inc=1, device_id=peer, device_id_type=MESH)
+
+    def clear_plane(buffer, index):
+        for part in range(PARTS):
+            buffer[index, part, TOP : TOP + ROWS, :] = jnp.zeros((ROWS, LANES), jnp.float32)
+
+    clear_plane(field, 0)
+    clear_plane(field, PLANES + 1)
+
+    def rows_of(buffer, k, row):
+        start = (k * CHUNK + 1) * PARTS * PADDED + row
+        return buffer.reshape((PLANES + 2) * PARTS * PADDED, LANES).at[pl.ds(start, STRIP, stride=PADDED), :]
+
+    for k in range(CHUNKS):
+        for row in (TOP - 1, TOP + ROWS):
+            rows_of(field, k, row)[...] = jnp.zeros((STRIP, LANES), jnp.float32)
     pl.semaphore_wait(barrier, len(peers))
 
     def remote(src, dst, send, recv, to):
@@ -86,50 +114,34 @@
     def plane_of(buffer, index):
         return buffer.at[index, :, pl.ds(TOP, ROWS), :]
 
-    def x_faces(buffer, send, recv):
-        low = remote(plane_of(buffer, 1), plane_of(buffer, PLANES + 1), send.at[0], recv.at[0], down_x)
-        high = remote(plane_of(buffer, PLANES), plane_of(buffer, 0), send.at[1], recv.at[1], up_x)
-        return low, high
-
     def y_faces(faces, halo, send, recv, k):
-        rows = pl.ds(k * CHUNK * PARTS, CHUNK * PARTS)
+        rows = pl.ds(k * STRIP, STRIP)
         low = remote(faces.at[0, rows], halo.at[1, rows], send.at[0, k], recv.at[0, k], down_y)
         high = remote(faces.at[1, rows], halo.at[0, rows], send.at[1, k], recv.at[1, k], up_y)
         return low, high
 
-    s_low, s_high = x_faces(field, xs_send, xs_recv)
-    m_low, m_high = x_faces(middle, xm_send, xm_recv)
+    s_low = remote(plane_of(field, 1), beside_x.at[1], xs_send.at[0], xs_recv.at[0], down_x)
+    s_high = remote(plane_of(field, PLANES), beside_x.at[0], xs_send.at[1], xs_recv.at[1], up_x)
+    m_low = remote(plane_of(middle, 1), plane_of(middle, PLANES + 1), xm_send.at[0], xm_recv.at[0], down_x)
+    m_high = remote(plane_of(middle, PLANES), plane_of(middle, 0), xm_send.at[1], xm_recv.at[1], up_x)
 
     def send_faces(k):
         for part in range(PARTS):
             load(k, part).wait()
-        for i in range(CHUNK):
-            for part in range(PARTS):
-                at = pl.ds((k * CHUNK + i) * PARTS + part, 1)
-                faces_s[0, at, :] = field[k * CHUNK + i + 1, part, TOP : TOP + 1, :]
-                faces_s[1, at, :] = field[k * CHUNK + i + 1, part, TOP + ROWS - 1 : TOP + ROWS, :]
+        faces_s[0, pl.ds(k * STRIP, STRIP), :] = rows_of(field, k, TOP)[...]
+        faces_s[1, pl.ds(k * STRIP, STRIP), :] = rows_of(field, k, TOP + ROWS - 1)[...]
         for copy in y_faces(faces_s, halo_s, fs_send, fs_recv, k):
             copy.start()
 
     send_faces(7)
     s_high.start()
-    send_faces(0)
-    s_low.start()
     send_faces(6)
-
-    def rest(k, carry):
-        send_faces(k)
-        return carry
-
-    lax.fori_loop(1, 6, rest, 0)
 
     fx_copies = [
         remote(fx_all.at[core, zl], fx_all.at[core, zl], fx_send.at[i], fx_recv.at[i], to)
         for i, to in enumerate(fx_peers)
     ]
     fx_load.wait()
-    for copy in fx_copies:
-        copy.start()
     fz_load.wait()
     fy_load.wait()
     eye = (
@@ -144,12 +156,6 @@
 
     lane = lax.broadcasted_iota(jnp.int32, (BAND, LANES), 1)
     at_left, at_right = lane == 0, lane == LANES - 1
-
-    def fill_halo(buffer, halo, plane):
-        for part in range(PARTS):
-            at = pl.ds(plane * PARTS + part, 1)
-            buffer[plane + 1, part, TOP - 1 : TOP, :] = jnp.where(gy > 0, halo[0, at, :], 0.0)
-            buffer[plane + 1, part, TOP + ROWS : TOP + ROWS + 1, :] = jnp.where(gy < 7, halo[1, at, :], 0.0)
 
     def stepped(buffer, plane, row):
         at = plane + 1
@@ -172,46 +178,42 @@
             results.append((1.0 - 6.0 * spread_rate) * c + spread_rate * beside + source)
         return results
 
-    def clear_plane(buffer, index):
-        for part in range(PARTS):
-            buffer[index, part, TOP : TOP + ROWS, :] = jnp.zeros((ROWS, LANES), jnp.float32)
-
     def first_stage(k):
         load_pref(k).wait()
-        low, high = y_faces(faces_s, halo_s, fs_send, fs_recv, k)
-        low.wait_recv()
-        high.wait_recv()
-
-        @pl.when(k == CHUNKS - 1)
-        def _():
-            s_low.wait_recv()
-
-            @pl.when(gx == 15)
-            def _():
-                clear_plane(field, PLANES + 1)
-
-        @pl.when(k == 0)
-        def _():
-            s_high.wait_recv()
-
-            @pl.when(gx == 0)
-            def _():
-                clear_plane(field, 0)
 
         def plane_step(i, carry):
             plane = k * CHUNK + i
-            fill_halo(field, halo_s, plane)
             for row in range(0, ROWS, BAND):
                 for part, value in enumerate(stepped(field, plane, row)):
                     middle[plane + 1, part, TOP + row : TOP + row + BAND, :] = value
-                    at = pl.ds(plane * PARTS + part, 1)
-                    if row == 0:
-                        faces_m[0, at, :] = value[0:1, :]
-                    if row == ROWS - BAND:
-                        faces_m[1, at, :] = value[BAND - 1 : BAND, :]
             return carry
 
         lax.fori_loop(0, CHUNK, plane_step, 0)
+
+    def add_x(plane, side, inside):
+        for part in range(PARTS):
+            own = (plane + 1, part, slice(TOP, TOP + ROWS), slice(None))
+            middle[own] = middle[own] + spread_rate * jnp.where(inside, beside_x[side, part], 0.0)
+
+    def add_halo(k):
+        @pl.when(k == CHUNKS - 1)
+        def _():
+            s_low.wait_recv()
+            add_x(PLANES - 1, 1, gx < 15)
+
+        @pl.when(k == 0)
+        def _():
+            s_high.wait_recv()
+            add_x(0, 0, gx > 0)
+
+        for copy in y_faces(faces_s, halo_s, fs_send, fs_recv, k):
+            copy.wait_recv()
+        rows = pl.ds(k * STRIP, STRIP)
+        for side, inside, row in ((0, gy > 0, TOP), (1, gy < 7, TOP + ROWS - 1)):
+            edge = rows_of(middle, k, row)
+            value = edge[...] + spread_rate * jnp.where(inside, halo_s[side, rows, :], 0.0)
+            faces_m[side, rows, :] = value
+            edge[...] = value
         for copy in y_faces(faces_m, halo_m, fm_send, fm_recv, k):
             copy.start()
 
@@ -264,9 +266,12 @@
             def _():
                 clear_plane(middle, 0)
 
+        rows = pl.ds(k * STRIP, STRIP)
+        rows_of(middle, k, TOP - 1)[...] = jnp.where(gy > 0, halo_m[0, rows, :], 0.0)
+        rows_of(middle, k, TOP + ROWS)[...] = jnp.where(gy < 7, halo_m[1, rows, :], 0.0)
+
         def plane_step(i, carry):
             plane = k * CHUNK + i
-            fill_halo(middle, halo_m, plane)
             for row in range(0, ROWS, BAND):
                 for part, value in enumerate(stepped(middle, plane, row)):
                     value = 0.5 * (field[plane + 1, part, TOP + row : TOP + row + BAND, :] + value)
@@ -332,15 +337,27 @@
         fx_t[...] = jnp.concatenate([high, high, low], axis=1)
 
     def step(t, carry):
+        pl.when(t < CHUNKS - 2)(lambda: send_faces(t))
+
+        @pl.when(t == 0)
+        def _():
+            s_low.start()
+
+        @pl.when(t == 3)
+        def _():
+            for copy in fx_copies:
+                copy.start()
+
         pl.when(t < CHUNKS)(lambda: first_stage((t + CHUNKS - 1) % CHUNKS))
-        pl.when((t >= 2) & (t < CHUNKS + 2))(lambda: second_stage(t - 2))
-        pl.when(t == CHUNKS + 1)(prepare_x)
-        pl.when((t >= 4) & (t < CHUNKS + 4))(lambda: y_first_done(t - 4))
-        pl.when((t >= 6) & (t < CHUNKS + 6))(lambda: y_second_done(t - 6))
-        pl.when(t >= 8)(lambda: z_done(t - 8))
+        pl.when((t >= FIX) & (t < CHUNKS + FIX))(lambda: add_halo((t - FIX + CHUNKS - 1) % CHUNKS))
+        pl.when((t >= SECOND) & (t < CHUNKS + SECOND))(lambda: second_stage(t - SECOND))
+        pl.when((t >= FIRST_SUM) & (t < CHUNKS + FIRST_SUM))(lambda: y_first_done(t - FIRST_SUM))
+        pl.when((t >= SECOND_SUM) & (t < CHUNKS + SECOND_SUM))(lambda: y_second_done(t - SECOND_SUM))
+        pl.when(t == CHUNKS + SECOND)(prepare_x)
+        pl.when(t >= Z_SUM)(lambda: z_done(t - Z_SUM))
         return carry
 
-    lax.fori_loop(0, CHUNKS + 8, step, 0)
+    lax.fori_loop(0, CHUNKS + Z_SUM, step, 0)
 
     for k in range(CHUNKS):
         core_copy(k).wait_recv()
@@ -383,7 +400,7 @@
     f32, bf16 = jnp.float32, jnp.bfloat16
     dma = pltpu.SemaphoreType.DMA
     vmem = pltpu.VMEM
-    padded = vmem((PLANES + 2, PARTS, ROWS + 16, LANES), f32)
+    padded = vmem((PLANES + 2, PARTS, PADDED, LANES), f32)
     faces = vmem((2, PLANES * PARTS, LANES), f32)
     anywhere = pl.BlockSpec(memory_space=pl.ANY)
     return pl.pallas_call(
@@ -395,7 +412,7 @@
         in_specs=[anywhere] * 5,
         out_specs=(pl.BlockSpec(memory_space=vmem), pl.BlockSpec(memory_space=vmem)),
         scratch_shapes=[
-            padded, padded, vmem((PLANES, ROWS, PARTS * LANES), f32), vmem((CHUNK, ROWS, PARTS * LANES), bf16),
+            padded, padded, vmem((PLANES, ROWS, PARTS * LANES), f32), vmem((2, PARTS, ROWS, LANES), f32), vmem((CHUNK, ROWS, PARTS * LANES), bf16),
             vmem((512, 128), bf16), vmem((64, 64), f32), vmem((2, 2, 64, 512), f32),
             vmem((64, 192), bf16), vmem((128, 768), bf16),
             faces, faces, faces, faces,
@@ -408,9 +425,9 @@
             dma((3,)), dma((3,)), dma((CHUNKS, 2)), dma((CHUNKS, 2)), dma((CHUNKS, 2)), dma((CHUNKS, 2)),
             dma((CHUNKS, 3)), dma((CHUNKS, 3)), dma((CHUNKS,)), dma((CHUNKS,)), dma((3,)), dma((3,)),
         ],
-        compiler_params=pltpu.CompilerParams(collective_id=0, has_side_effects=True, vmem_limit_bytes=50 << 20),
+        compiler_params=pltpu.CompilerParams(collective_id=0, has_side_effects=True, vmem_limit_bytes=40 << 20),
         name="heun_tucker",
-    )(scalar, prefactor, factor_x, factor_y, factor_z)
+    )(scalar, prefactor, *(pltpu.with_memory_space_constraint(a, pltpu.HBM) for a in (factor_x, factor_y, factor_z)))
 
 
 def solution(mesh):

time: 87.1 us -> 67 us (0.77)
  Pallas kernels: 74.4 us -> 62.2 us
  local copies, waits for them, and re-layouts: 11.8 us -> 4.05 us
    pallas_call x1, Pallas kernels: 74.4 us -> 62.2 us  [on_device(): pl.pallas_call(kernel, out_shape=(jax.ShapeDtypeStruct((PLANES, ROWS, PAR...]
    unnamed x8 -> x2, local copies, waits for them, and re-layouts: 11.8 us -> 4.05 us
where the time goes in v2:
time: 67 us; the launch traced here: 66.9 us
  Pallas kernels  62.2 us (93%)
  local copies, waits for them, and re-layouts  4.05 us (6%)
    pallas_call x1, Pallas kernels, on_device(): pl.pallas_call(kernel, out_shape=(jax.ShapeDtypeStruct((PLANES, ROWS, PAR...  62.2 us
    unnamed x2, local copies, waits for them, and re-layouts  4.05 us

profile of v2, /device:TPU:1, one launch (start us, length us, event | category | flops | bytes accessed | tf_op | source)
XLA Modules:
  0.0 66.9 jit_solution(17475117717061344625)
XLA Ops:
  0.6 62.2 %heun_tucker.1 = (f32[64,64,512]{2,1,0:T(8,128)S(1)}, f32[32,8,128]{2,1,0:T(8,128)S(1)}) custom-call(f32[64,64,512]{2,1,0:T(8,128)} %scalar.1, f32[64,64,512]{2,1,0:T(8,128)} %prefactor.1, f32[64,512]{1,0:T(8,128)} %factor_x.1, f32[64,64]{1,0:T(8,128)} %factor_y.1, bf16[512,128]{1,0:T(8,128)(2,1)} %factor_z.1), custom_call_target="tpu_custom_call" | custom-call | tf_op jit(solution)/shard_map/heun_tucker/pallas_call | solution.py:406
  62.9 3.4 %copy.9 = f32[64,64,512]{2,1,0:T(8,128)} copy(f32[64,64,512]{2,1,0:T(8,128)S(1)} %get-tuple-element.4) | data formatting | bytes 16777216
  66.3 0.7 copy.10

commit v3 on v2

--- a/solution.py
+++ b/solution.py
@@ -14,6 +14,7 @@
 TOP = 8
 PADDED = ROWS + 16
 STRIP = CHUNK * PARTS
+GROUP = 8
 BAND = 16
 FIX = 4
 SECOND = 8
@@ -28,7 +29,7 @@
 
 def kernel(
     scalar, prefactor, factor_x, factor_y, factor_z, advanced, core_out,
-    field, middle, pref, beside_x, lowered, fz, fy, fx_all, fy_t, fx_t,
+    field, middle, pref, beside_x, band, lowered, fz, fy, fx_all, fy_t, fx_t,
     faces_s, halo_s, faces_m, halo_m,
     y_red, y_in1, y_in2, z_in, gathered, x_out, x_in,
     load_sem, pref_sem, small_sem,
@@ -104,6 +105,9 @@
     for k in range(CHUNKS):
         for row in (TOP - 1, TOP + ROWS):
             rows_of(field, k, row)[...] = jnp.zeros((STRIP, LANES), jnp.float32)
+    along = lax.broadcasted_iota(jnp.int32, (512, 512), 0)
+    across = lax.broadcasted_iota(jnp.int32, (512, 512), 1)
+    band[...] = ((along == across + 1) | (across == along + 1)).astype(jnp.bfloat16)
     pl.semaphore_wait(barrier, len(peers))
 
     def remote(src, dst, send, recv, to):
@@ -154,25 +158,27 @@
     )
     fy_t[...] = jnp.concatenate([fy_high, fy_high, fy_low], axis=1)
 
-    lane = lax.broadcasted_iota(jnp.int32, (BAND, LANES), 1)
-    at_left, at_right = lane == 0, lane == LANES - 1
-
-    def stepped(buffer, plane, row):
+    def beside_z(buffer, plane):
+        planes = [
+            jnp.concatenate([buffer[plane + i + 1, part, TOP : TOP + ROWS, :] for part in range(PARTS)], axis=1)
+            for i in range(GROUP)
+        ]
+        return jnp.dot(
+            jnp.concatenate(planes, axis=0).astype(jnp.bfloat16), band[...], preferred_element_type=jnp.float32
+        )
+
+    def stepped(buffer, plane, row, sums):
         at = plane + 1
         own = slice(TOP + row, TOP + row + BAND)
         centers = [buffer[at, part, own, :] for part in range(PARTS)]
-        lefts = [pltpu.roll(c, 1, 1) for c in centers]
-        rights = [pltpu.roll(c, LANES - 1, 1) for c in centers]
         results = []
         for part, c in enumerate(centers):
-            left = jnp.where(at_left, lefts[part - 1] if part > 0 else 0.0, lefts[part])
-            right = jnp.where(at_right, rights[part + 1] if part + 1 < PARTS else 0.0, rights[part])
             beside = buffer[at + 1, part, own, :] + buffer[at - 1, part, own, :]
             beside = beside + (
                 buffer[at, part, TOP + row + 1 : TOP + row + 1 + BAND, :]
                 + buffer[at, part, TOP + row - 1 : TOP + row - 1 + BAND, :]
             )
-            beside = beside + (left + right)
+            beside = beside + sums[row : row + BAND, part * LANES : (part + 1) * LANES]
             factor = pref[plane, row : row + BAND, part * LANES : (part + 1) * LANES]
             source = factor * jnp.exp(-activation / (1.0 + c * c))
             results.append((1.0 - 6.0 * spread_rate) * c + spread_rate * beside + source)
@@ -181,14 +187,17 @@
     def first_stage(k):
         load_pref(k).wait()
 
-        def plane_step(i, carry):
-            plane = k * CHUNK + i
-            for row in range(0, ROWS, BAND):
-                for part, value in enumerate(stepped(field, plane, row)):
-                    middle[plane + 1, part, TOP + row : TOP + row + BAND, :] = value
+        def group_step(g, carry):
+            start = k * CHUNK + g * GROUP
+            sums = beside_z(field, start)
+            for i in range(GROUP):
+                plane = start + i
+                for row in range(0, ROWS, BAND):
+                    for part, value in enumerate(stepped(field, plane, row, sums[i * ROWS : (i + 1) * ROWS])):
+                        middle[plane + 1, part, TOP + row : TOP + row + BAND, :] = value
             return carry
 
-        lax.fori_loop(0, CHUNK, plane_step, 0)
+        lax.fori_loop(0, CHUNK // GROUP, group_step, 0)
 
     def add_x(plane, side, inside):
         for part in range(PARTS):
@@ -270,17 +279,20 @@
         rows_of(middle, k, TOP - 1)[...] = jnp.where(gy > 0, halo_m[0, rows, :], 0.0)
         rows_of(middle, k, TOP + ROWS)[...] = jnp.where(gy < 7, halo_m[1, rows, :], 0.0)
 
-        def plane_step(i, carry):
-            plane = k * CHUNK + i
-            for row in range(0, ROWS, BAND):
-                for part, value in enumerate(stepped(middle, plane, row)):
-                    value = 0.5 * (field[plane + 1, part, TOP + row : TOP + row + BAND, :] + value)
-                    lanes = slice(part * LANES, (part + 1) * LANES)
-                    advanced[plane, row : row + BAND, lanes] = value
-                    lowered[i, row : row + BAND, lanes] = value.astype(jnp.bfloat16)
+        def group_step(g, carry):
+            start = k * CHUNK + g * GROUP
+            sums = beside_z(middle, start)
+            for i in range(GROUP):
+                plane = start + i
+                for row in range(0, ROWS, BAND):
+                    for part, value in enumerate(stepped(middle, plane, row, sums[i * ROWS : (i + 1) * ROWS])):
+                        value = 0.5 * (field[plane + 1, part, TOP + row : TOP + row + BAND, :] + value)
+                        lanes = slice(part * LANES, (part + 1) * LANES)
+                        advanced[plane, row : row + BAND, lanes] = value
+                        lowered[g * GROUP + i, row : row + BAND, lanes] = value.astype(jnp.bfloat16)
             return carry
 
-        lax.fori_loop(0, CHUNK, plane_step, 0)
+        lax.fori_loop(0, CHUNK // GROUP, group_step, 0)
         z_red = jnp.dot(
             lowered[...].reshape(CHUNK * ROWS, PARTS * LANES), fz[...], preferred_element_type=jnp.float32
         )
@@ -359,6 +371,15 @@
 
     lax.fori_loop(0, CHUNKS + Z_SUM, step, 0)
 
+    def x_pair(b):
+        rows = pl.ds(b, 2)
+        return [
+            remote(
+                x_out.at[(x + 1 + i) % 4, rows], x_in.at[i, rows], xr_send.at[i, b // 2], xr_recv.at[i, b // 2], to
+            )
+            for i, to in enumerate(x_peers)
+        ]
+
     for k in range(CHUNKS):
         core_copy(k).wait_recv()
     for b in range(0, 8, 2):
@@ -371,15 +392,14 @@
         for owner in range(4):
             for j in range(2):
                 x_out[owner, b + j] = both[owner * 32 : owner * 32 + 32, j * LANES : (j + 1) * LANES]
-    x_copies = [
-        remote(x_out.at[(x + 1 + i) % 4], x_in.at[i], xr_send.at[i], xr_recv.at[i], to) for i, to in enumerate(x_peers)
-    ]
-    for copy in x_copies:
-        copy.start()
-    for copy in x_copies:
-        copy.wait_recv()
-    for b in range(8):
-        core_out[:, b, :] = (x_out[x, b] + x_in[0, b]) + (x_in[1, b] + x_in[2, b])
+        for copy in x_pair(b):
+            copy.start()
+    for b in range(0, 8, 2):
+        for copy in x_pair(b):
+            copy.wait_recv()
+        for j in (b, b + 1):
+            core_out[:, j, :] = (x_out[x, j] + x_in[0, j]) + (x_in[1, j] + x_in[2, j])
+    x_copies = [copy for b in range(0, 8, 2) for copy in x_pair(b)]
 
     for copy in (s_low, s_high, m_low, m_high, *fx_copies, *x_copies):
         copy.wait_send()
@@ -412,7 +432,7 @@
         in_specs=[anywhere] * 5,
         out_specs=(pl.BlockSpec(memory_space=vmem), pl.BlockSpec(memory_space=vmem)),
         scratch_shapes=[
-            padded, padded, vmem((PLANES, ROWS, PARTS * LANES), f32), vmem((2, PARTS, ROWS, LANES), f32), vmem((CHUNK, ROWS, PARTS * LANES), bf16),
+            padded, padded, vmem((PLANES, ROWS, PARTS * LANES), f32), vmem((2, PARTS, ROWS, LANES), f32), vmem((512, 512), bf16), vmem((CHUNK, ROWS, PARTS * LANES), bf16),
             vmem((512, 128), bf16), vmem((64, 64), f32), vmem((2, 2, 64, 512), f32),
             vmem((64, 192), bf16), vmem((128, 768), bf16),
             faces, faces, faces, faces,
@@ -423,7 +443,7 @@
             dma((2, CHUNKS)), dma((2, CHUNKS)), dma((2, CHUNKS)), dma((2, CHUNKS)),
             dma((2,)), dma((2,)), dma((2,)), dma((2,)),
             dma((3,)), dma((3,)), dma((CHUNKS, 2)), dma((CHUNKS, 2)), dma((CHUNKS, 2)), dma((CHUNKS, 2)),
-            dma((CHUNKS, 3)), dma((CHUNKS, 3)), dma((CHUNKS,)), dma((CHUNKS,)), dma((3,)), dma((3,)),
+            dma((CHUNKS, 3)), dma((CHUNKS, 3)), dma((CHUNKS,)), dma((CHUNKS,)), dma((3, 4)), dma((3, 4)),
         ],
         compiler_params=pltpu.CompilerParams(collective_id=0, has_side_effects=True, vmem_limit_bytes=40 << 20),
         name="heun_tucker",

time: 67 us -> 63.5 us (0.948)
  Pallas kernels: 62.2 us -> 58.7 us
    pallas_call x1, Pallas kernels: 62.2 us -> 58.7 us  [on_device(): pl.pallas_call(kernel, out_shape=(jax.ShapeDtypeStruct((PLANES, ROWS, PAR...]
where the time goes in v3:
time: 63.5 us; the launch traced here: 63.4 us
  Pallas kernels  58.7 us (92%)
  local copies, waits for them, and re-layouts  4.05 us (6%)
  between operations  0.64 us (1%)
    pallas_call x1, Pallas kernels, on_device(): pl.pallas_call(kernel, out_shape=(jax.ShapeDtypeStruct((PLANES, ROWS, PAR...  58.7 us
    unnamed x2, local copies, waits for them, and re-layouts  4.05 us

profile of v3, /device:TPU:1, one launch (start us, length us, event | category | flops | bytes accessed | tf_op | source)
XLA Modules:
  0.0 63.4 jit_solution(15024700994387988993)
XLA Ops:
  0.6 58.7 %heun_tucker.1 = (f32[64,64,512]{2,1,0:T(8,128)S(1)}, f32[32,8,128]{2,1,0:T(8,128)S(1)}) custom-call(f32[64,64,512]{2,1,0:T(8,128)} %scalar.1, f32[64,64,512]{2,1,0:T(8,128)} %prefactor.1, f32[64,512]{1,0:T(8,128)} %factor_x.1, f32[64,64]{1,0:T(8,128)} %factor_y.1, bf16[512,128]{1,0:T(8,128)(2,1)} %factor_z.1), custom_call_target="tpu_custom_call" | custom-call | tf_op jit(solution)/shard_map/heun_tucker/pallas_call | solution.py:426
  59.3 3.4 %copy.9 = f32[64,64,512]{2,1,0:T(8,128)} copy(f32[64,64,512]{2,1,0:T(8,128)S(1)} %get-tuple-element.4) | data formatting | bytes 16777216
  62.7 0.7 %copy.10 = f32[32,8,128]{2,1,0:T(8,128)} copy(f32[32,8,128]{2,1,0:T(8,128)S(1)} %get-tuple-element.5) | data formatting | bytes 262144

commit v4 on v3

--- a/solution.py
+++ b/solution.py
@@ -16,8 +16,8 @@
 STRIP = CHUNK * PARTS
 GROUP = 8
 BAND = 16
-FIX = 4
-SECOND = 8
+FIX = 2
+SECOND = 7
 FIRST_SUM, SECOND_SUM, Z_SUM = SECOND + 2, SECOND + 4, SECOND + 6
 
 
@@ -64,27 +64,17 @@
         rows = pl.ds(k * CHUNK, CHUNK)
         return pltpu.make_async_copy(prefactor.at[rows], pref.at[rows], pref_sem.at[k])
 
-    for part in range(PARTS):
-        load(7, part).start()
-        load(6, part).start()
-    load_pref(7).start()
-    for k in (0, 1):
+    for k in (7, 0, 6, 1, 2, 3, 4, 5):
         for part in range(PARTS):
             load(k, part).start()
+    load_pref(7).start()
     load_pref(0).start()
     fx_load = pltpu.make_async_copy(factor_x, fx_all.at[core, zl], small_sem.at[0])
     fz_load = pltpu.make_async_copy(factor_z, fz, small_sem.at[1])
     fy_load = pltpu.make_async_copy(factor_y, fy, small_sem.at[2])
-    for k in range(2, CHUNKS - 2):
-        for part in range(PARTS):
-            load(k, part).start()
-        load_pref(k - 1).start()
-        if k == 2:
-            fx_load.start()
-            fz_load.start()
-            fy_load.start()
-    load_pref(5).start()
-    load_pref(6).start()
+    fx_load.start()
+    fz_load.start()
+    fy_load.start()
 
     barrier = pltpu.get_barrier_semaphore()
     peers = [up_x, down_x, up_y, down_y, pair_a, pair_b, *z_peers, partner, fx_peers[2], *x_peers]
@@ -139,7 +129,14 @@
 
     send_faces(7)
     s_high.start()
-    send_faces(6)
+    send_faces(0)
+    s_low.start()
+
+    def other_faces(k, carry):
+        send_faces(k)
+        return carry
+
+    lax.fori_loop(1, CHUNKS - 1, other_faces, 0)
 
     fx_copies = [
         remote(fx_all.at[core, zl], fx_all.at[core, zl], fx_send.at[i], fx_recv.at[i], to)
@@ -297,16 +294,16 @@
             lowered[...].reshape(CHUNK * ROWS, PARTS * LANES), fz[...], preferred_element_type=jnp.float32
         )
         blocks = [y, y_by1, (y + 2) % 4, y_by3]
-        for i in range(0, CHUNK, 2):
-            pair = jnp.concatenate([z_red[i * ROWS : (i + 1) * ROWS], z_red[(i + 1) * ROWS : (i + 2) * ROWS]], axis=1)
-            high, low = split(pair)
-            stacked = jnp.concatenate([high, low, high], axis=0)
-            both = jnp.dot(fy_t[...], stacked, preferred_element_type=jnp.float32)
-            for owner in range(8):
-                for j in range(2):
-                    y_red[k, blocks[owner % 4], owner // 4, i + j] = both[
-                        owner * 8 : owner * 8 + 8, j * LANES : (j + 1) * LANES
-                    ]
+        planes = jnp.concatenate([z_red[i * ROWS : (i + 1) * ROWS] for i in range(CHUNK)], axis=1)
+        high, low = split(planes)
+        both = jnp.dot(
+            fy_t[...], jnp.concatenate([high, low, high], axis=0), preferred_element_type=jnp.float32
+        )
+        for owner in range(8):
+            for i in range(CHUNK):
+                y_red[k, blocks[owner % 4], owner // 4, i] = both[
+                    owner * 8 : owner * 8 + 8, i * LANES : (i + 1) * LANES
+                ]
         for copy in y_first(k):
             copy.start()
 
@@ -349,11 +346,7 @@
         fx_t[...] = jnp.concatenate([high, high, low], axis=1)
 
     def step(t, carry):
-        pl.when(t < CHUNKS - 2)(lambda: send_faces(t))
-
-        @pl.when(t == 0)
-        def _():
-            s_low.start()
+        pl.when(t < CHUNKS - 2)(lambda: load_pref(t + 1).start())
 
         @pl.when(t == 3)
         def _():
@@ -364,8 +357,8 @@
         pl.when((t >= FIX) & (t < CHUNKS + FIX))(lambda: add_halo((t - FIX + CHUNKS - 1) % CHUNKS))
         pl.when((t >= SECOND) & (t < CHUNKS + SECOND))(lambda: second_stage(t - SECOND))
         pl.when((t >= FIRST_SUM) & (t < CHUNKS + FIRST_SUM))(lambda: y_first_done(t - FIRST_SUM))
+        pl.when(t == CHUNKS + FIRST_SUM - 1)(prepare_x)
         pl.when((t >= SECOND_SUM) & (t < CHUNKS + SECOND_SUM))(lambda: y_second_done(t - SECOND_SUM))
-        pl.when(t == CHUNKS + SECOND)(prepare_x)
         pl.when(t >= Z_SUM)(lambda: z_done(t - Z_SUM))
         return carry
 

time: 63.5 us -> 62.7 us (0.987)
  Pallas kernels: 58.7 us -> 57.9 us
    pallas_call x1, Pallas kernels: 58.7 us -> 57.9 us  [on_device(): pl.pallas_call(kernel, out_shape=(jax.ShapeDtypeStruct((PLANES, ROWS, PAR...]
where the time goes in v4:
time: 62.7 us; the launch traced here: 62.6 us
  Pallas kernels  57.9 us (92%)
  local copies, waits for them, and re-layouts  4.05 us (6%)
  between operations  0.64 us (1%)
    pallas_call x1, Pallas kernels, on_device(): pl.pallas_call(kernel, out_shape=(jax.ShapeDtypeStruct((PLANES, ROWS, PAR...  57.9 us
    unnamed x2, local copies, waits for them, and re-layouts  4.05 us

profile of v4, /device:TPU:1, one launch (start us, length us, event | category | flops | bytes accessed | tf_op | source)
XLA Modules:
  0.0 62.6 jit_solution(5959944895714606945)
XLA Ops:
  0.6 57.9 %heun_tucker.1 = (f32[64,64,512]{2,1,0:T(8,128)S(1)}, f32[32,8,128]{2,1,0:T(8,128)S(1)}) custom-call(f32[64,64,512]{2,1,0:T(8,128)} %scalar.1, f32[64,64,512]{2,1,0:T(8,128)} %prefactor.1, f32[64,512]{1,0:T(8,128)} %factor_x.1, f32[64,64]{1,0:T(8,128)} %factor_y.1, bf16[512,128]{1,0:T(8,128)(2,1)} %factor_z.1), custom_call_target="tpu_custom_call" | custom-call | tf_op jit(solution)/shard_map/heun_tucker/pallas_call | solution.py:419
  58.6 3.4 %copy.9 = f32[64,64,512]{2,1,0:T(8,128)} copy(f32[64,64,512]{2,1,0:T(8,128)S(1)} %get-tuple-element.4) | data formatting | bytes 16777216
  62.0 0.7 %copy.10 = f32[32,8,128]{2,1,0:T(8,128)} copy(f32[32,8,128]{2,1,0:T(8,128)S(1)} %get-tuple-element.5) | data formatting | bytes 262144
